TPU v7x, 32 devices: a whole 2x2x4 slice. The times are simulated.
32 devices in a mesh: seq: 8 (over z, y), feat: 4 (over x, core).
Axes of the slice: x: 2, y: 2, z: 4, core: 2. Of those that a mesh axis runs over, the one named last changes fastest.
Arguments:
- activations_in: bfloat16 [6144, 512], P('seq', 'feat'), may hold values from -6 to 6
- cotangent: bfloat16 [6144, 512], P('seq', 'feat'), may hold values from -6 to 6
- seq_start: int32 [16], P('seq'), may hold values from 0 to 768, as said below
- seq_length: int32 [16], P('seq'), may hold values from 0 to 768, as said below
- input_matrix: float32 [2, 512, 768], P(None, 'feat'), may hold values from -0.25 to 0.25
- output_matrix: float32 [2, 1536, 512], P(None, None, 'feat'), may hold values from -1.25 to 1.25
- gate_matrix: float32 [2, 512, 512], P(None, None, 'feat'), may hold values from -0.25 to 0.25
- feature_vectors: float32 [2, 4, 512], P(None, None, 'feat'), may hold values from 0.1 to 1.9
- state_vectors: float32 [2, 3, 384], replicated, may hold values from -20 to 20, as said below
- velocity_input: float32 [2, 512, 768], P(None, 'feat'), may hold values from -6 to 6
- velocity_output: float32 [2, 1536, 512], P(None, None, 'feat'), may hold values from -6 to 6
- velocity_gate: float32 [2, 512, 512], P(None, None, 'feat'), may hold values from -6 to 6
- velocity_feature: float32 [2, 4, 512], P(None, None, 'feat'), may hold values from -6 to 6
- velocity_state: float32 [2, 3, 384], replicated, may hold values from -6 to 6
- average_input: float32 [2, 512, 768], P(None, 'feat'), may hold values from -0.25 to 0.25
- average_output: float32 [2, 1536, 512], P(None, None, 'feat'), may hold values from -1.25 to 1.25
- average_gate: float32 [2, 512, 512], P(None, None, 'feat'), may hold values from -0.25 to 0.25
- average_feature: float32 [2, 4, 512], P(None, None, 'feat'), may hold values from 0.1 to 1.9
- average_state: float32 [2, 3, 384], replicated, may hold values from -3 to 1
Outputs:
- activations_out: float32 [6144, 512], P('seq', 'feat')
- input_gradient: float32 [6144, 512], P('seq', 'feat')
- gradient_input: float32 [2, 512, 768], P(None, 'feat')
- gradient_output: float32 [2, 1536, 512], P(None, None, 'feat')
- gradient_gate: float32 [2, 512, 512], P(None, None, 'feat')
- gradient_feature: float32 [2, 4, 512], P(None, None, 'feat')
- gradient_state: float32 [2, 3, 384], replicated
- updated_input: float32 [2, 512, 768], P(None, 'feat')
- updated_output: float32 [2, 1536, 512], P(None, None, 'feat')
- updated_gate: float32 [2, 512, 512], P(None, None, 'feat')
- updated_feature: float32 [2, 4, 512], P(None, None, 'feat')
- state_change: float32 [2, 3, 384], replicated
- momentum_input: float32 [2, 512, 768], P(None, 'feat')
- momentum_output: float32 [2, 1536, 512], P(None, None, 'feat')
- momentum_gate: float32 [2, 512, 512], P(None, None, 'feat')
- momentum_feature: float32 [2, 4, 512], P(None, None, 'feat')
- momentum_state: float32 [2, 3, 384], replicated
- smoothed_input: float32 [2, 512, 768], P(None, 'feat')
- smoothed_output: float32 [2, 1536, 512], P(None, None, 'feat')
- smoothed_gate: float32 [2, 512, 512], P(None, None, 'feat')
- smoothed_feature: float32 [2, 4, 512], P(None, None, 'feat')
- smoothed_state: float32 [2, 3, 384], replicated
Inputs may be any that keep to these rules, and one draw needn't show every extreme that they name: `seq_length`: sequences of a device lie in its own buffer, ordered and without intersection; one device holds a single sequence of 768 tokens and an empty slot, every other device two sequences of 192 to 384 tokens. `seq_start`: positions within a device's buffer; a slot of length zero starts at 768. `state_vectors`: rows hold log(-Re Lambda), Im Lambda and the log timestep.
All inputs are finite; a program needn't handle non-finite values.
Results may differ from a plain program's by a relative error of at most 0.012.
The roundings to bfloat16 on the way count: a program that leaves them out, or rounds other values in their place, can miss the bound.
Values may be sent and summed in bfloat16 or wider, within the bound.
A program may use at most 448 MiB of HBM per device.

v0:
```python
import math
import jax
import jax.numpy as jnp
from jax import lax
from jax.sharding import PartitionSpec as P

epsilon = 1e-05
momentum = 0.9
smoothing = 0.5
slow_rate = 0.02
main_rate = 0.05
weight_decay = 0.1


def smooth(value):
    return jax.nn.gelu(value, approximate=False)


def combine(earlier, later):
    mult_real = later[0] * earlier[0] - later[1] * earlier[1]
    mult_imag = later[0] * earlier[1] + later[1] * earlier[0]
    add_real = later[0] * earlier[2] - later[1] * earlier[3] + later[2]
    add_imag = later[0] * earlier[3] + later[1] * earlier[2] + later[3]
    return (mult_real, mult_imag, add_real, add_imag)


def masks_of(starts, lengths, count):
    position = jnp.arange(count, dtype=jnp.int32)[:, None]
    begin = starts[None, :]
    finish = begin + lengths[None, :]
    inside = (position >= begin) & (position < finish)
    alive = jnp.any(inside, 1)
    opening = jnp.any(inside & (position == begin), 1)
    closing = jnp.any(inside & (position == finish - 1), 1)
    return (
        alive.astype(jnp.float32),
        (alive & ~opening).astype(jnp.float32),
        (alive & ~closing).astype(jnp.float32),
    )


def prefix(current, backward):
    length = current[2].shape[0]
    offset = 1
    while offset < length:

        def shifted(value):
            filler = jnp.zeros((offset,) + value.shape[1:], value.dtype)
            if backward:
                return jnp.concatenate([value[offset:], filler], 0)
            return jnp.concatenate([filler, value[: length - offset]], 0)

        earlier = tuple((shifted(value) for value in current))
        current = combine(earlier, current)
        offset = offset * 2
    return current


def scan_states(drive, state_row, alive, carry_prev, carry_next):
    width = state_row.shape[1]
    rate = -jnp.exp(state_row[0])
    frequency = state_row[1]
    timestep = jnp.exp(state_row[2])
    decay = jnp.exp(rate * timestep)
    angle = frequency * timestep
    pole_real = decay * jnp.cos(angle)
    pole_imag = decay * jnp.sin(angle)
    denom = rate * rate + frequency * frequency
    factor_real = ((pole_real - 1.0) * rate + pole_imag * frequency) / denom
    factor_imag = (pole_imag * rate - (pole_real - 1.0) * frequency) / denom
    drive_real = drive[:, :width]
    drive_imag = drive[:, width:]
    input_real = (drive_real * factor_real - drive_imag * factor_imag) * alive[:, None]
    input_imag = (drive_real * factor_imag + drive_imag * factor_real) * alive[:, None]
    ahead = prefix(
        (carry_prev[:, None] * pole_real, carry_prev[:, None] * pole_imag, input_real, input_imag),
        False,
    )
    behind = prefix(
        (carry_next[:, None] * pole_real, carry_next[:, None] * pole_imag, input_real, input_imag),
        True,
    )
    return jnp.concatenate([ahead[2], ahead[3], behind[2], behind[3]], 1)


def update(weight, gradient, velocity, average, rate, decay):
    adjusted = gradient + decay * weight
    velocity_new = momentum * velocity + adjusted
    change = -rate * (adjusted + momentum * velocity_new)
    weight_new = weight + change
    average_new = smoothing * average + (1.0 - smoothing) * weight_new
    return (weight_new, velocity_new, average_new, change)


def contract_rows(left, right):
    return lax.dot_general(
        left, right, (((0,), (0,)), ((), ())), preferred_element_type=jnp.float32
    )


def contract_cols(left, right):
    return lax.dot_general(
        left, right, (((1,), (1,)), ((), ())), preferred_element_type=jnp.float32
    )


def moments(stream):
    whole = lax.all_gather(stream, "feat", axis=1, tiled=True)
    center = jnp.mean(whole, 1, keepdims=True)
    spread = whole - center
    variance = jnp.mean(spread * spread, 1, keepdims=True)
    return (center, lax.rsqrt(variance + epsilon))


def back_moments(unit_grad, unit):
    spread_grad, crossed = (
        lax.all_gather(unit_grad, "feat", axis=1, tiled=True),
        lax.all_gather(unit_grad * unit, "feat", axis=1, tiled=True),
    )
    return (jnp.mean(spread_grad, 1, keepdims=True), jnp.mean(crossed, 1, keepdims=True))


def state_forward(normed_low, in_low, state_row, masks):
    partial_drive = jnp.dot(normed_low, in_low, preferred_element_type=jnp.float32)
    drive = lax.psum(partial_drive, "feat")
    states = scan_states(drive, state_row, masks[0], masks[1], masks[2])
    return (drive, states.astype(jnp.bfloat16))


def state_backward(drive, state_row, masks, mixed_low, out_low):

    def scanned(drive_in, rows_in):
        return scan_states(drive_in, rows_in, masks[0], masks[1], masks[2])

    partial_states = contract_cols(mixed_low, out_low)
    states_grad = lax.psum(partial_states, "feat")
    unused, pull = jax.vjp(scanned, drive, state_row)
    drive_grad, row_grad = pull(states_grad)
    return (drive_grad.astype(jnp.bfloat16), row_grad)


def body(
    activations_in,
    cotangent,
    seq_start,
    seq_length,
    input_matrix,
    output_matrix,
    gate_matrix,
    feature_vectors,
    state_vectors,
    velocity_input,
    velocity_output,
    velocity_gate,
    velocity_feature,
    velocity_state,
    average_input,
    average_output,
    average_gate,
    average_feature,
    average_state,
):
    count = activations_in.shape[0]
    layers = input_matrix.shape[0]
    masks = masks_of(seq_start, seq_length, count)
    stream = activations_in.astype(jnp.float32)
    saved = []
    for layer in range(layers):
        in_low = input_matrix[layer].astype(jnp.bfloat16)
        out_low = output_matrix[layer].astype(jnp.bfloat16)
        gate_low = gate_matrix[layer].astype(jnp.bfloat16)
        feature_row = feature_vectors[layer]
        center, scale = moments(stream)
        unit = (stream - center) * scale
        normed = unit * feature_row[0] + feature_row[1]
        normed_low = normed.astype(jnp.bfloat16)
        drive, states_low = state_forward(normed_low, in_low, state_vectors[layer], masks)
        mixed = (
            jnp.dot(states_low, out_low, preferred_element_type=jnp.float32)
            + feature_row[2] * normed
        )
        act = smooth(mixed)
        act_all = lax.all_gather(act.astype(jnp.bfloat16), "feat", axis=1, tiled=True)
        pre = jnp.dot(act_all, gate_low, preferred_element_type=jnp.float32) + feature_row[3]
        saved.append((scale, unit, normed, normed_low, drive, states_low, mixed, act, act_all, pre))
        stream = stream + act * jax.nn.sigmoid(pre)
    grad = cotangent.astype(jnp.float32) * masks[0][:, None]
    layer_grads = [None] * layers
    for layer in reversed(range(layers)):
        scale, unit, normed, normed_low, drive, states_low, mixed, act, act_all, pre = saved[layer]
        in_low = input_matrix[layer].astype(jnp.bfloat16)
        out_low = output_matrix[layer].astype(jnp.bfloat16)
        gate_low = gate_matrix[layer].astype(jnp.bfloat16)
        feature_row = feature_vectors[layer]
        gate = jax.nn.sigmoid(pre)
        pre_grad = (grad * act * gate * (1.0 - gate)).astype(jnp.bfloat16)
        gate_grad = contract_rows(act_all, pre_grad)
        gate_bias_grad = jnp.sum(pre_grad.astype(jnp.float32), 0)
        act_grad = grad * gate + lax.psum_scatter(
            contract_cols(pre_grad, gate_low), "feat", scatter_dimension=1, tiled=True
        )
        mixed_grad = jax.vjp(smooth, mixed)[1](act_grad)[0]
        skip_grad = jnp.sum(mixed_grad * normed, 0)
        mixed_low = mixed_grad.astype(jnp.bfloat16)
        out_grad = contract_rows(states_low, mixed_low)
        drive_low, row_grad = state_backward(drive, state_vectors[layer], masks, mixed_low, out_low)
        in_grad = contract_rows(normed_low, drive_low)
        normed_grad = mixed_grad * feature_row[2] + contract_cols(drive_low, in_low)
        gain_grad = jnp.sum(normed_grad * unit, 0)
        bias_grad = jnp.sum(normed_grad, 0)
        unit_grad = normed_grad * feature_row[0]
        first_mean, second_mean = back_moments(unit_grad, unit)
        grad = grad + scale * (unit_grad - first_mean - unit * second_mean)
        feature_grad = jnp.stack([gain_grad, bias_grad, skip_grad, gate_bias_grad])
        layer_grads[layer] = (in_grad, out_grad, gate_grad, feature_grad, row_grad)
    stacked_in = jnp.stack([entry[0] for entry in layer_grads])
    stacked_out = jnp.stack([entry[1] for entry in layer_grads])
    stacked_gate = jnp.stack([entry[2] for entry in layer_grads])
    stacked_feature = jnp.stack([entry[3] for entry in layer_grads])
    stacked_state = jnp.stack([entry[4] for entry in layer_grads])
    summed = lax.psum(
        (stacked_in, stacked_out, stacked_gate, stacked_feature, stacked_state), "seq"
    )
    factor = 1.0 / math.sqrt(count * lax.axis_size("seq"))
    grad_in = summed[0] * factor
    grad_out = summed[1] * factor
    grad_gate = summed[2] * factor
    grad_feature = summed[3] * factor
    grad_state = summed[4] * factor
    new_in = update(input_matrix, grad_in, velocity_input, average_input, slow_rate, 0.0)
    new_out = update(output_matrix, grad_out, velocity_output, average_output, slow_rate, 0.0)
    new_gate = update(gate_matrix, grad_gate, velocity_gate, average_gate, main_rate, weight_decay)
    new_feature = update(
        feature_vectors, grad_feature, velocity_feature, average_feature, main_rate, weight_decay
    )
    new_state = update(state_vectors, grad_state, velocity_state, average_state, slow_rate, 0.0)
    return (
        stream,
        grad,
        grad_in,
        grad_out,
        grad_gate,
        grad_feature,
        grad_state,
        new_in[0],
        new_out[0],
        new_gate[0],
        new_feature[0],
        new_state[3],
        new_in[1],
        new_out[1],
        new_gate[1],
        new_feature[1],
        new_state[1],
        new_in[2],
        new_out[2],
        new_gate[2],
        new_feature[2],
        new_state[2],
    )


def solution(mesh):
    return jax.shard_map(
        body,
        mesh=mesh,
        in_specs=(
            P("seq", "feat"),
            P("seq", "feat"),
            P("seq"),
            P("seq"),
            P(None, "feat", None),
            P(None, None, "feat"),
            P(None, None, "feat"),
            P(None, None, "feat"),
            P(),
            P(None, "feat", None),
            P(None, None, "feat"),
            P(None, None, "feat"),
            P(None, None, "feat"),
            P(),
            P(None, "feat", None),
            P(None, None, "feat"),
            P(None, None, "feat"),
            P(None, None, "feat"),
            P(),
        ),
        out_specs=(
            P("seq", "feat"),
            P("seq", "feat"),
            P(None, "feat", None),
            P(None, None, "feat"),
            P(None, None, "feat"),
            P(None, None, "feat"),
            P(),
            P(None, "feat", None),
            P(None, None, "feat"),
            P(None, None, "feat"),
            P(None, None, "feat"),
            P(),
            P(None, "feat", None),
            P(None, None, "feat"),
            P(None, None, "feat"),
            P(None, None, "feat"),
            P(),
            P(None, "feat", None),
            P(None, None, "feat"),
            P(None, None, "feat"),
            P(None, None, "feat"),
            P(),
        ),
        check_vma=False,
    )
```

profile of v0, /device:TPU:0, one launch (start us, length us, event | category | flops | bytes accessed | tf_op | source)
XLA Modules:
  0.0 1222.3 jit_solution(16966885579422786372)
XLA Ops:
  10.5 22.2 %all-gather.7.cloned.1.call-done = f32[768,512]{1,0:T(8,128)} async-done(((f32[768,128]{1,0:T(8,128)}), f32[768,512]{1,0:T(8,128)}) %all-gather.7.cloned.1.call-update) | async-done | bytes 1572880 | tf_op jit(solution)/shard_map/all_gather | solution.py:108
  43.4 52.2 %all-reduce.322.cloned.1.call-done = f32[768,768]{1,0:T(8,128)} async-done(((f32[768,768]{1,0:T(8,128)}), f32[768,768]{1,0:T(8,128)}) %all-reduce.322.cloned.1.call-update) | async-done | bytes 2359312 | tf_op jit(solution)/shard_map/psum | solution.py:125
  154.0 8.2 all_gather.25
  164.5 20.4 %all-gather.9.cloned.1.call-done = f32[768,512]{1,0:T(8,128)} async-done(((f32[768,128]{1,0:T(8,128)}), f32[768,512]{1,0:T(8,128)}) %all-gather.9.cloned.1.call-update) | async-done | bytes 1572880 | tf_op jit(solution)/shard_map/all_gather | solution.py:108
  192.1 55.7 %all-reduce.324.cloned.1.call-done = f32[768,768]{1,0:T(8,128)} async-done(((f32[768,768]{1,0:T(8,128)}), f32[768,768]{1,0:T(8,128)}) %all-reduce.324.cloned.1.call-update) | async-done | bytes 2359312 | tf_op jit(solution)/shard_map/psum | solution.py:125
  306.8 8.2 all_gather.27
  320.8 28.8 %reduce-scatter.3.cloned.1.call-done = f32[768,128]{1,0:T(8,128)} async-done(((f32[768,512]{1,0:T(8,128)}), f32[768,128]{1,0:T(8,128)}) %reduce-scatter.3.cloned.1.call-update) | async-done | bytes 393232 | tf_op jit(solution)/shard_map/reduce_scatter | solution.py:199
  352.9 3.9 fusion.341
  357.1 93.9 %all-reduce.326.cloned.1.call-done = f32[768,1536]{1,0:T(8,128)} async-done(((f32[768,1536]{1,0:T(8,128)}), f32[768,1536]{1,0:T(8,128)}) %all-reduce.326.cloned.1.call-update) | async-done | bytes 4718608 | tf_op jit(solution)/shard_map/psum | solution.py:136
  451.0 5.1 fusion.478
  461.9 5.8 fusion.447
  494.6 4.0 fusion.445
  517.8 4.0 fusion.432
  528.8 4.2 fusion.431
  562.2 3.8 fusion.430
  586.3 4.0 fusion.441
  599.9 4.0 fusion.440
  611.9 3.9 fusion.439
  659.7 19.4 %all-gather.13.cloned.1.call-done = f32[768,512]{1,0:T(8,128)} async-done(((f32[768,128]{1,0:T(8,128)}), f32[768,512]{1,0:T(8,128)}) %all-gather.13.cloned.1.call-update) | async-done | bytes 1572880 | tf_op jit(solution)/shard_map/all_gather | solution.py:118
  680.7 20.4 %all-gather.11.cloned.1.call-done = f32[768,512]{1,0:T(8,128)} async-done(((f32[768,128]{1,0:T(8,128)}), f32[768,512]{1,0:T(8,128)}) %all-gather.11.cloned.1.call-update) | async-done | bytes 1572880 | tf_op jit(solution)/shard_map/all_gather | solution.py:117
  707.7 28.3 %reduce-scatter.5.cloned.1.call-done = f32[768,128]{1,0:T(8,128)} async-done(((f32[768,512]{1,0:T(8,128)}), f32[768,128]{1,0:T(8,128)}) %reduce-scatter.5.cloned.1.call-update) | async-done | bytes 393232 | tf_op jit(solution)/shard_map/reduce_scatter | solution.py:199
  737.9 3.9 fusion.340
  742.3 93.7 %all-reduce.328.cloned.1.call-done = f32[768,1536]{1,0:T(8,128)} async-done(((f32[768,1536]{1,0:T(8,128)}), f32[768,1536]{1,0:T(8,128)}) %all-reduce.328.cloned.1.call-update) | async-done | bytes 4718608 | tf_op jit(solution)/shard_map/psum | solution.py:136
  836.0 4.8 fusion.477
  846.5 5.0 fusion.423
  904.8 3.9 fusion.407
  952.5 3.9 fusion.405
  964.5 4.0 fusion.417
  978.2 4.0 fusion.416
  990.1 3.9 fusion.415
  1049.8 37.1 %all-reduce.314 = (f32[2,4,128]{2,1,0:T(4,128)S(1)}, f32[2,3,384]{2,1,0:T(4,128)S(1)}) all-reduce(f32[2,4,128]{2,1,0:T(4,128)S(1)} %pad_maximum_fusion.10, f32[2,3,384]{2,1,0:T(4,128)S(1)} %pad_maximum_fusion.9), channel_id=1, replica_groups=mesh['seq'=8,'feat'=4] {'seq'}, use_global_device_ids=true, to_apply=%region_28.0 | all-reduce | flops 3328 | bytes 26624 | tf_op jit(solution)/shard_map/psum | solution.py:221
  1095.4 110.1 %all-reduce.330.cloned.1.call-done = (f32[2,128,768]{2,1,0:T(8,128)}, f32[2,1536,128]{2,1,0:T(8,128)}, f32[2,512,128]{2,1,0:T(8,128)}) async-done(((f32[2,128,768]{2,1,0:T(8,128)}, f32[2,1536,128]{2,1,0:T(8,128)}, f32[2,512,128]{2,1,0:T(8,128)}), (f32[2,128,768]{2,1,0:T(8,128)}, f32[2,1536,128]{2,1,0:T(8,128)}, f32[2,512,128]{2,1,0:T(8,128)})) %all-reduce.330.cloned.1.call-update) | async-done | bytes 2883600 | tf_op jit(solution)/shard_map/psum | solution.py:221
  (1629 shorter events, 527.1 us)
Async XLA Ops:
  7.2 25.5 %all-gather.7.cloned.1.call-start = ((), (), s32[]{:S(2)}) async-start(), calls=%async_computation.2 | async-start | bytes 1966080 | tf_op jit(solution)/shard_map/all_gather | solution.py:108
  9.0 86.5 %all-reduce.322.cloned.1.call-start = ((), (), s32[]{:S(2)}) async-start(), calls=%async_computation.3 | async-start | bytes 4718592 | tf_op jit(solution)/shard_map/psum | solution.py:125
  39.8 145.1 %all-gather.9.cloned.1.call-start = ((), (), s32[]{:S(2)}) async-start(), calls=%async_computation.4 | async-start | bytes 1966080 | tf_op jit(solution)/shard_map/all_gather | solution.py:108
  43.4 54.2 %copy-start.553 = (f32[384]{0:T(512)}, f32[384]{0:T(512)S(1)}, u32[]{:S(2)}) copy-start(f32[384]{0:T(512)S(1)} %get-tuple-element.706) | copy-start | bytes 4612
  43.4 54.2 %copy-start.555 = (f32[384]{0:T(512)}, f32[384]{0:T(512)S(1)}, u32[]{:S(2)}) copy-start(f32[384]{0:T(512)S(1)} %get-tuple-element.707) | copy-start | bytes 4612
  100.3 27.3 %copy-start.16 = (f32[768,384]{1,0:T(8,128)}, f32[768,384]{1,0:T(8,128)S(1)}, u32[]{:S(2)}) copy-start(f32[768,384]{1,0:T(8,128)S(1)} %get-tuple-element.600) | copy-start | bytes 3538948
  100.3 27.3 %copy-start.20 = (f32[768,384]{1,0:T(8,128)}, f32[768,384]{1,0:T(8,128)S(1)}, u32[]{:S(2)}) copy-start(f32[768,384]{1,0:T(8,128)S(1)} %get-tuple-element.599) | copy-start | bytes 3538948
  164.4 83.3 %all-reduce.324.cloned.1.call-start = ((), (), s32[]{:S(2)}) async-start(), calls=%async_computation.5 | async-start | bytes 4718592 | tf_op jit(solution)/shard_map/psum | solution.py:125
  192.0 157.6 %reduce-scatter.3.cloned.1.call-start = ((), (), s32[]{:S(2)}) async-start(), calls=%async_computation.6 | async-start | bytes 1966080 | tf_op jit(solution)/shard_map/reduce_scatter | solution.py:199
  192.1 57.7 %copy-start.557 = (f32[384]{0:T(512)}, f32[384]{0:T(512)S(1)}, u32[]{:S(2)}) copy-start(f32[384]{0:T(512)S(1)} %get-tuple-element.700) | copy-start | bytes 4612
  192.1 57.7 %copy-start.559 = (f32[384]{0:T(512)}, f32[384]{0:T(512)S(1)}, u32[]{:S(2)}) copy-start(f32[384]{0:T(512)S(1)} %get-tuple-element.701) | copy-start | bytes 4612
  253.7 27.3 %copy-start.18 = (f32[768,384]{1,0:T(8,128)}, f32[768,384]{1,0:T(8,128)S(1)}, u32[]{:S(2)}) copy-start(f32[768,384]{1,0:T(8,128)S(1)} %get-tuple-element.602) | copy-start | bytes 3538948
  253.7 27.3 %copy-start.22 = (f32[768,384]{1,0:T(8,128)}, f32[768,384]{1,0:T(8,128)S(1)}, u32[]{:S(2)}) copy-start(f32[768,384]{1,0:T(8,128)S(1)} %get-tuple-element.601) | copy-start | bytes 3538948
  320.8 130.2 %all-reduce.326.cloned.1.call-start = ((), (), s32[]{:S(2)}) async-start(), calls=%async_computation.7 | async-start | bytes 9437184 | tf_op jit(solution)/shard_map/psum | solution.py:136
  356.8 322.2 %all-gather.13.cloned.1.call-start = ((), (), s32[]{:S(2)}) async-start(), calls=%async_computation.9 | async-start | bytes 1966080 | tf_op jit(solution)/shard_map/all_gather | solution.py:118
  658.9 42.2 %all-gather.11.cloned.1.call-start = ((), (), s32[]{:S(2)}) async-start(), calls=%async_computation.8 | async-start | bytes 1966080 | tf_op jit(solution)/shard_map/all_gather | solution.py:117
  659.6 76.4 %reduce-scatter.5.cloned.1.call-start = ((), (), s32[]{:S(2)}) async-start(), calls=%async_computation.10 | async-start | bytes 1966080 | tf_op jit(solution)/shard_map/reduce_scatter | solution.py:199
  704.6 31.4 %copy-start.498 = (f32[768,128]{1,0:T(8,128)}, f32[768,128]{1,0:T(8,128)S(1)}, u32[]{:S(2)}) copy-start(f32[768,128]{1,0:T(8,128)S(1)} %get-tuple-element.286) | copy-start | bytes 1179652
  707.7 128.3 %all-reduce.328.cloned.1.call-start = ((), (), s32[]{:S(2)}) async-start(), calls=%async_computation.11 | async-start | bytes 9437184 | tf_op jit(solution)/shard_map/psum | solution.py:136
  741.8 94.2 %copy-start.450 = (f32[256,384]{1,0:T(8,128)S(1)}, f32[256,384]{1,0:T(8,128)}, u32[]{:S(2)}) copy-start(f32[256,384]{1,0:T(8,128)} %copy-done.449) | copy-start | bytes 1179652
  741.8 94.2 %copy-start.452 = (f32[256,384]{1,0:T(8,128)S(1)}, f32[256,384]{1,0:T(8,128)}, u32[]{:S(2)}) copy-start(f32[256,384]{1,0:T(8,128)} %copy-done.451) | copy-start | bytes 1179652
  741.8 348.1 %all-gather.17.cloned.1.call-start = ((), (), s32[]{:S(2)}) async-start(), calls=%async_computation.13 | async-start | bytes 1966080 | tf_op jit(solution)/shard_map/all_gather | solution.py:118
  1035.7 55.9 %all-gather.15.cloned.1.call-start = ((), (), s32[]{:S(2)}) async-start(), calls=%async_computation.12 | async-start | bytes 1966080 | tf_op jit(solution)/shard_map/all_gather | solution.py:117
  1036.3 169.1 %all-reduce.330.cloned.1.call-start = ((), (), s32[]{:S(2)}) async-start(), calls=%async_computation.14 | async-start | bytes 5767168 | tf_op jit(solution)/shard_map/psum | solution.py:221
  1048.5 38.4 %copy-start.563 = (f32[2,3,384]{2,0,1:T(2,128)S(1)}, f32[2,3,384]{2,0,1:T(2,128)}, u32[]{:S(2)}) copy-start(f32[2,3,384]{2,0,1:T(2,128)} %param.37) | copy-start | bytes 27652
  1048.5 38.4 %copy-start.564 = (f32[2,3,384]{2,0,1:T(2,128)S(1)}, f32[2,3,384]{2,0,1:T(2,128)}, u32[]{:S(2)}) copy-start(f32[2,3,384]{2,0,1:T(2,128)} %param.32) | copy-start | bytes 27652
  1048.5 40.8 %copy-start.562 = (f32[2,4,128]{2,1,0:T(4,128)S(1)}, f32[2,4,128]{2,1,0:T(4,128)}, u32[]{:S(2)}) copy-start(f32[2,4,128]{2,1,0:T(4,128)} %param.26) | copy-start | bytes 12292
  1048.5 40.8 %copy-start.577 = (f32[2,4,128]{2,1,0:T(4,128)S(1)}, f32[2,4,128]{2,1,0:T(4,128)}, u32[]{:S(2)}) copy-start(f32[2,4,128]{2,1,0:T(4,128)} %param.36) | copy-start | bytes 12292
  1048.5 40.8 %copy-start.578 = (f32[2,4,128]{2,1,0:T(4,128)S(1)}, f32[2,4,128]{2,1,0:T(4,128)}, u32[]{:S(2)}) copy-start(f32[2,4,128]{2,1,0:T(4,128)} %param.31) | copy-start | bytes 12292
  1091.6 113.9 %copy-start.515 = (f32[2,512,128]{2,1,0:T(8,128)S(1)}, f32[2,512,128]{2,1,0:T(8,128)}, u32[]{:S(2)}) copy-start(f32[2,512,128]{2,1,0:T(8,128)} %param.25) | copy-start | bytes 1572868
  1091.6 113.9 %copy-start.547 = (f32[2,512,128]{2,1,0:T(8,128)S(1)}, f32[2,512,128]{2,1,0:T(8,128)}, u32[]{:S(2)}) copy-start(f32[2,512,128]{2,1,0:T(8,128)} %param.35) | copy-start | bytes 1572868
  1091.6 113.9 %copy-start.548 = (f32[2,512,128]{2,1,0:T(8,128)S(1)}, f32[2,512,128]{2,1,0:T(8,128)}, u32[]{:S(2)}) copy-start(f32[2,512,128]{2,1,0:T(8,128)} %param.30) | copy-start | bytes 1572868
  (573 other events, 1549.8 us)
Sparse Core Ops, SparseCore 0:
  10.2 22.5 all-gather.6
  39.9 55.6 all-reduce.321
  164.6 20.2 all-gather.8
  192.1 55.6 all-reduce.323
  320.9 28.6 reduce-scatter.2
  356.9 94.0 all-reduce.325
  659.0 19.9 all-gather.12
  681.2 19.8 all-gather.10
  707.8 28.1 reduce-scatter.4
  742.0 94.0 all-reduce.327
  1035.9 19.9 all-gather.16
  1057.9 19.8 all-gather.14
  1082.3 123.1 all-reduce.329
where the time goes:
time: 1230 us; the launch traced here: 1220 us
  waiting for transfers between devices  546 us (44%)
  other arithmetic  391 us (32%)
  local copies, waits for them, and re-layouts  167 us (14%)
  blocking collectives  53.4 us (4%)
  matrix products  42.7 us (3%)
  between operations  20.4 us (2%)
    psum x2, waiting for transfers between devices, state_backward(): states_grad = lax.psum(partial_states, 'feat')  188 us
    unnamed x1188, local copies, waits for them, and re-layouts  153 us
    neg x32, other arithmetic, combine(): mult_real = later[0] * earlier[0] - later[1] * earlier[1]  115 us
    psum x1, waiting for transfers between devices, body(): lax.psum((stacked_in, stacked_out, stacked_gate, stacked_feature, stacked...  110 us
    psum x2, waiting for transfers between devices, state_forward(): drive = lax.psum(partial_drive, 'feat')  108 us
    add_any x40, other arithmetic, combine(): add_real = later[0] * earlier[2] - later[1] * earlier[3] + later[2]  59.8 us
    neg x36, other arithmetic, combine(): add_real = later[0] * earlier[2] - later[1] * earlier[3] + later[2]  58.3 us
    reduce_scatter x2, waiting for transfers between devices, body(): lax.psum_scatter(contract_cols(pre_grad, gate_low), 'feat', scatter_dimen...  57 us
  transfers between devices with their start and end apart: 13, of which 11 were waited for; matrix products, arithmetic and copies ran while one was open for 2% of the time, Pallas kernels for 0%

commit v1 on v0

--- a/solution.py
+++ b/solution.py
@@ -105,7 +105,8 @@
 
 
 def moments(stream):
-    whole = lax.all_gather(stream, "feat", axis=1, tiled=True)
+    sent = jnp.stack([stream] * lax.axis_size("feat"))
+    whole = jnp.concatenate(lax.all_to_all(sent, "feat", 0, 0), axis=1)
     center = jnp.mean(whole, 1, keepdims=True)
     spread = whole - center
     variance = jnp.mean(spread * spread, 1, keepdims=True)

time: 1230 us -> 1230 us (level)
  blocking collectives: 53.4 us -> 75.9 us
  waiting for transfers between devices: 546 us -> 524 us
    all_gather x2 -> x0, waiting for transfers between devices: 42.6 us -> none  [moments(): whole = lax.all_gather(stream, 'feat', axis=1, tiled=True)]
    all_to_all x0 -> x1, blocking collectives: none -> 22.5 us  [moments(): whole = jnp.concatenate(lax.all_to_all(sent, 'feat', 0, 0), axis=1)]
    all_to_all x0 -> x1, waiting for transfers between devices: none -> 18.7 us  [moments(): whole = jnp.concatenate(lax.all_to_all(sent, 'feat', 0, 0), axis=1)]
    unnamed x1188 -> x1184, local copies, waits for them, and re-layouts: 153 us -> 153 us
  transfers between devices with their start and end apart: 13 -> 12, of which waited for: 11 -> 10; matrix products, arithmetic and copies ran while one was open for 2% -> 2% of each run, Pallas kernels for 0% -> 0%
where the time goes in v1:
time: 1230 us; the launch traced here: 1220 us
  waiting for transfers between devices  524 us (43%)
  other arithmetic  386 us (31%)
  local copies, waits for them, and re-layouts  169 us (14%)
  blocking collectives  75.9 us (6%)
  matrix products  42.6 us (3%)
  between operations  20.2 us (2%)
    psum x2, waiting for transfers between devices, state_backward(): states_grad = lax.psum(partial_states, 'feat')  188 us
    unnamed x1184, local copies, waits for them, and re-layouts  153 us
    neg x32, other arithmetic, combine(): mult_real = later[0] * earlier[0] - later[1] * earlier[1]  115 us
    psum x1, waiting for transfers between devices, body(): lax.psum((stacked_in, stacked_out, stacked_gate, stacked_feature, stacked...  110 us
    psum x2, waiting for transfers between devices, state_forward(): drive = lax.psum(partial_drive, 'feat')  109 us
    add_any x40, other arithmetic, combine(): add_real = later[0] * earlier[2] - later[1] * earlier[3] + later[2]  59.9 us
    neg x36, other arithmetic, combine(): add_real = later[0] * earlier[2] - later[1] * earlier[3] + later[2]  58.3 us
    reduce_scatter x2, waiting for transfers between devices, body(): lax.psum_scatter(contract_cols(pre_grad, gate_low), 'feat', scatter_dimen...  57 us
  transfers between devices with their start and end apart: 12, of which 10 were waited for; matrix products, arithmetic and copies ran while one was open for 2% of the time, Pallas kernels for 0%

profile of v1, /device:TPU:0, one launch (start us, length us, event | category | flops | bytes accessed | tf_op | source)
XLA Modules:
  0.0 1222.6 jit_solution(17021295266570212307)
XLA Ops:
  9.4 4.3 all-to-all-start
  15.1 18.7 %all-to-all-done = f32[4,768,128]{2,1,0:T(8,128)S(1)} async-done(((f32[4,768,128]{2,1,0:T(8,128)}), f32[4,768,128]{2,1,0:T(8,128)S(1)}, u32[]{:S(2)}, u32[]{:S(2)}) %all-to-all-start) | async-done | bytes 1572896 | tf_op jit(solution)/shard_map/all_to_all | solution.py:109
  42.9 53.3 %all-reduce.322.cloned.1.call-done = f32[768,768]{1,0:T(8,128)} async-done(((f32[768,768]{1,0:T(8,128)}), f32[768,768]{1,0:T(8,128)}) %all-reduce.322.cloned.1.call-update) | async-done | bytes 2359312 | tf_op jit(solution)/shard_map/psum | solution.py:126
  154.4 8.2 all_gather.18
  164.8 22.5 %all_to_all.10 = f32[4,768,128]{2,1,0:T(8,128)S(1)} all-to-all(f32[4,768,128]{2,1,0:T(8,128)S(1)} %stack.90), channel_id=1, replica_groups=mesh['seq'=8,'feat'=4] {'feat'}, dimensions={0} | all-to-all | bytes 3145728 | tf_op jit(solution)/shard_map/all_to_all | solution.py:109
  193.0 55.7 %all-reduce.324.cloned.1.call-done = f32[768,768]{1,0:T(8,128)} async-done(((f32[768,768]{1,0:T(8,128)}), f32[768,768]{1,0:T(8,128)}) %all-reduce.324.cloned.1.call-update) | async-done | bytes 2359312 | tf_op jit(solution)/shard_map/psum | solution.py:126
  307.4 8.2 all_gather.19
  321.5 28.7 %reduce-scatter.3.cloned.1.call-done = f32[768,128]{1,0:T(8,128)} async-done(((f32[768,512]{1,0:T(8,128)}), f32[768,128]{1,0:T(8,128)}) %reduce-scatter.3.cloned.1.call-update) | async-done | bytes 393232 | tf_op jit(solution)/shard_map/reduce_scatter | solution.py:200
  353.6 3.9 fusion.341
  357.9 93.7 %all-reduce.326.cloned.1.call-done = f32[768,1536]{1,0:T(8,128)} async-done(((f32[768,1536]{1,0:T(8,128)}), f32[768,1536]{1,0:T(8,128)}) %all-reduce.326.cloned.1.call-update) | async-done | bytes 4718608 | tf_op jit(solution)/shard_map/psum | solution.py:137
  451.6 5.1 fusion.478
  462.6 5.8 fusion.447
  495.2 4.0 fusion.445
  518.4 4.0 fusion.432
  529.4 3.9 fusion.431
  586.6 4.0 fusion.441
  600.2 4.0 fusion.440
  612.2 3.9 fusion.439
  660.0 19.5 %all-gather.7.cloned.1.call-done = f32[768,512]{1,0:T(8,128)} async-done(((f32[768,128]{1,0:T(8,128)}), f32[768,512]{1,0:T(8,128)}) %all-gather.7.cloned.1.call-update) | async-done | bytes 1572880 | tf_op jit(solution)/shard_map/all_gather | solution.py:119
  681.2 20.2 %all-gather.5.cloned.1.call-done = f32[768,512]{1,0:T(8,128)} async-done(((f32[768,128]{1,0:T(8,128)}), f32[768,512]{1,0:T(8,128)}) %all-gather.5.cloned.1.call-update) | async-done | bytes 1572880 | tf_op jit(solution)/shard_map/all_gather | solution.py:118
  708.1 28.3 %reduce-scatter.5.cloned.1.call-done = f32[768,128]{1,0:T(8,128)} async-done(((f32[768,512]{1,0:T(8,128)}), f32[768,128]{1,0:T(8,128)}) %reduce-scatter.5.cloned.1.call-update) | async-done | bytes 393232 | tf_op jit(solution)/shard_map/reduce_scatter | solution.py:200
  738.3 3.9 fusion.340
  742.4 93.9 %all-reduce.328.cloned.1.call-done = f32[768,1536]{1,0:T(8,128)} async-done(((f32[768,1536]{1,0:T(8,128)}), f32[768,1536]{1,0:T(8,128)}) %all-reduce.328.cloned.1.call-update) | async-done | bytes 4718608 | tf_op jit(solution)/shard_map/psum | solution.py:137
  836.4 4.8 fusion.477
  846.9 5.0 fusion.423
  905.2 4.1 fusion.407
  953.1 3.9 fusion.405
  965.1 4.0 fusion.417
  978.7 4.0 fusion.416
  990.7 3.9 fusion.415
  1050.3 37.1 %all-reduce.314 = (f32[2,4,128]{2,1,0:T(4,128)S(1)}, f32[2,3,384]{2,1,0:T(4,128)S(1)}) all-reduce(f32[2,4,128]{2,1,0:T(4,128)S(1)} %pad_maximum_fusion.10, f32[2,3,384]{2,1,0:T(4,128)S(1)} %pad_maximum_fusion.9), channel_id=1, replica_groups=mesh['seq'=8,'feat'=4] {'seq'}, use_global_device_ids=true, to_apply=%region_28.0 | all-reduce | flops 3328 | bytes 26624 | tf_op jit(solution)/shard_map/psum | solution.py:222
  1095.8 110.2 %all-reduce.330.cloned.1.call-done = (f32[2,128,768]{2,1,0:T(8,128)}, f32[2,1536,128]{2,1,0:T(8,128)}, f32[2,512,128]{2,1,0:T(8,128)}) async-done(((f32[2,128,768]{2,1,0:T(8,128)}, f32[2,1536,128]{2,1,0:T(8,128)}, f32[2,512,128]{2,1,0:T(8,128)}), (f32[2,128,768]{2,1,0:T(8,128)}, f32[2,1536,128]{2,1,0:T(8,128)}, f32[2,512,128]{2,1,0:T(8,128)})) %all-reduce.330.cloned.1.call-update) | async-done | bytes 2883600 | tf_op jit(solution)/shard_map/psum | solution.py:222
  (1623 shorter events, 527.5 us)
Async XLA Ops:
  9.4 24.4 %all-to-all-start = ((f32[4,768,128]{2,1,0:T(8,128)}), f32[4,768,128]{2,1,0:T(8,128)S(1)}, u32[]{:S(2)}, u32[]{:S(2)}) async-start(f32[4,768,128]{2,1,0:T(8,128)} %stack.89), calls=%async_computation | async-start | bytes 3145728 | tf_op jit(solution)/shard_map/all_to_all | solution.py:109
  13.7 82.5 %all-reduce.322.cloned.1.call-start = ((), (), s32[]{:S(2)}) async-start(), calls=%async_computation.4 | async-start | bytes 4718592 | tf_op jit(solution)/shard_map/psum | solution.py:126
  39.3 209.4 %all-reduce.324.cloned.1.call-start = ((), (), s32[]{:S(2)}) async-start(), calls=%async_computation.5 | async-start | bytes 4718592 | tf_op jit(solution)/shard_map/psum | solution.py:126
  42.9 55.3 %copy-start.551 = (f32[384]{0:T(512)}, f32[384]{0:T(512)S(1)}, u32[]{:S(2)}) copy-start(f32[384]{0:T(512)S(1)} %get-tuple-element.706) | copy-start | bytes 4612
  42.9 55.3 %copy-start.553 = (f32[384]{0:T(512)}, f32[384]{0:T(512)S(1)}, u32[]{:S(2)}) copy-start(f32[384]{0:T(512)S(1)} %get-tuple-element.707) | copy-start | bytes 4612
  100.9 27.3 %copy-start.16 = (f32[768,384]{1,0:T(8,128)}, f32[768,384]{1,0:T(8,128)S(1)}, u32[]{:S(2)}) copy-start(f32[768,384]{1,0:T(8,128)S(1)} %get-tuple-element.600) | copy-start | bytes 3538948
  100.9 27.3 %copy-start.20 = (f32[768,384]{1,0:T(8,128)}, f32[768,384]{1,0:T(8,128)S(1)}, u32[]{:S(2)}) copy-start(f32[768,384]{1,0:T(8,128)S(1)} %get-tuple-element.599) | copy-start | bytes 3538948
  164.7 25.1 %copy-start.399 = (f32[768,128]{1,0:T(8,128)}, f32[768,128]{1,0:T(8,128)S(1)}, u32[]{:S(2)}) copy-start(f32[768,128]{1,0:T(8,128)S(1)} %get-tuple-element.726) | copy-start | bytes 1179652
  192.9 157.4 %reduce-scatter.3.cloned.1.call-start = ((), (), s32[]{:S(2)}) async-start(), calls=%async_computation.6 | async-start | bytes 1966080 | tf_op jit(solution)/shard_map/reduce_scatter | solution.py:200
  193.0 57.7 %copy-start.555 = (f32[384]{0:T(512)}, f32[384]{0:T(512)S(1)}, u32[]{:S(2)}) copy-start(f32[384]{0:T(512)S(1)} %get-tuple-element.700) | copy-start | bytes 4612
  193.0 57.7 %copy-start.557 = (f32[384]{0:T(512)}, f32[384]{0:T(512)S(1)}, u32[]{:S(2)}) copy-start(f32[384]{0:T(512)S(1)} %get-tuple-element.701) | copy-start | bytes 4612
  254.6 27.2 %copy-start.18 = (f32[768,384]{1,0:T(8,128)}, f32[768,384]{1,0:T(8,128)S(1)}, u32[]{:S(2)}) copy-start(f32[768,384]{1,0:T(8,128)S(1)} %get-tuple-element.602) | copy-start | bytes 3538948
  254.6 27.2 %copy-start.22 = (f32[768,384]{1,0:T(8,128)}, f32[768,384]{1,0:T(8,128)S(1)}, u32[]{:S(2)}) copy-start(f32[768,384]{1,0:T(8,128)S(1)} %get-tuple-element.601) | copy-start | bytes 3538948
  321.4 130.2 %all-reduce.326.cloned.1.call-start = ((), (), s32[]{:S(2)}) async-start(), calls=%async_computation.7 | async-start | bytes 9437184 | tf_op jit(solution)/shard_map/psum | solution.py:137
  357.5 322.0 %all-gather.7.cloned.1.call-start = ((), (), s32[]{:S(2)}) async-start(), calls=%async_computation.9 | async-start | bytes 1966080 | tf_op jit(solution)/shard_map/all_gather | solution.py:119
  659.3 42.1 %all-gather.5.cloned.1.call-start = ((), (), s32[]{:S(2)}) async-start(), calls=%async_computation.8 | async-start | bytes 1966080 | tf_op jit(solution)/shard_map/all_gather | solution.py:118
  659.9 76.4 %reduce-scatter.5.cloned.1.call-start = ((), (), s32[]{:S(2)}) async-start(), calls=%async_computation.10 | async-start | bytes 1966080 | tf_op jit(solution)/shard_map/reduce_scatter | solution.py:200
  704.9 31.4 %copy-start.496 = (f32[768,128]{1,0:T(8,128)}, f32[768,128]{1,0:T(8,128)S(1)}, u32[]{:S(2)}) copy-start(f32[768,128]{1,0:T(8,128)S(1)} %get-tuple-element.286) | copy-start | bytes 1179652
  708.0 128.3 %all-reduce.328.cloned.1.call-start = ((), (), s32[]{:S(2)}) async-start(), calls=%async_computation.11 | async-start | bytes 9437184 | tf_op jit(solution)/shard_map/psum | solution.py:137
  742.2 94.2 %copy-start.450 = (f32[256,384]{1,0:T(8,128)S(1)}, f32[256,384]{1,0:T(8,128)}, u32[]{:S(2)}) copy-start(f32[256,384]{1,0:T(8,128)} %copy-done.449) | copy-start | bytes 1179652
  742.2 94.2 %copy-start.452 = (f32[256,384]{1,0:T(8,128)S(1)}, f32[256,384]{1,0:T(8,128)}, u32[]{:S(2)}) copy-start(f32[256,384]{1,0:T(8,128)} %copy-done.451) | copy-start | bytes 1179652
  742.2 348.3 %all-gather.11.cloned.1.call-start = ((), (), s32[]{:S(2)}) async-start(), calls=%async_computation.13 | async-start | bytes 1966080 | tf_op jit(solution)/shard_map/all_gather | solution.py:119
  1036.3 55.8 %all-gather.9.cloned.1.call-start = ((), (), s32[]{:S(2)}) async-start(), calls=%async_computation.12 | async-start | bytes 1966080 | tf_op jit(solution)/shard_map/all_gather | solution.py:118
  1036.9 169.1 %all-reduce.330.cloned.1.call-start = ((), (), s32[]{:S(2)}) async-start(), calls=%async_computation.14 | async-start | bytes 5767168 | tf_op jit(solution)/shard_map/psum | solution.py:222
  1049.0 38.4 %copy-start.561 = (f32[2,3,384]{2,0,1:T(2,128)S(1)}, f32[2,3,384]{2,0,1:T(2,128)}, u32[]{:S(2)}) copy-start(f32[2,3,384]{2,0,1:T(2,128)} %param.37) | copy-start | bytes 27652
  1049.0 38.4 %copy-start.562 = (f32[2,3,384]{2,0,1:T(2,128)S(1)}, f32[2,3,384]{2,0,1:T(2,128)}, u32[]{:S(2)}) copy-start(f32[2,3,384]{2,0,1:T(2,128)} %param.32) | copy-start | bytes 27652
  1049.0 40.8 %copy-start.560 = (f32[2,4,128]{2,1,0:T(4,128)S(1)}, f32[2,4,128]{2,1,0:T(4,128)}, u32[]{:S(2)}) copy-start(f32[2,4,128]{2,1,0:T(4,128)} %param.26) | copy-start | bytes 12292
  1049.0 40.8 %copy-start.575 = (f32[2,4,128]{2,1,0:T(4,128)S(1)}, f32[2,4,128]{2,1,0:T(4,128)}, u32[]{:S(2)}) copy-start(f32[2,4,128]{2,1,0:T(4,128)} %param.36) | copy-start | bytes 12292
  1049.1 40.8 %copy-start.576 = (f32[2,4,128]{2,1,0:T(4,128)S(1)}, f32[2,4,128]{2,1,0:T(4,128)}, u32[]{:S(2)}) copy-start(f32[2,4,128]{2,1,0:T(4,128)} %param.31) | copy-start | bytes 12292
  1092.1 114.0 %copy-start.513 = (f32[2,512,128]{2,1,0:T(8,128)S(1)}, f32[2,512,128]{2,1,0:T(8,128)}, u32[]{:S(2)}) copy-start(f32[2,512,128]{2,1,0:T(8,128)} %param.25) | copy-start | bytes 1572868
  1092.1 114.0 %copy-start.545 = (f32[2,512,128]{2,1,0:T(8,128)S(1)}, f32[2,512,128]{2,1,0:T(8,128)}, u32[]{:S(2)}) copy-start(f32[2,512,128]{2,1,0:T(8,128)} %param.35) | copy-start | bytes 1572868
  1092.1 113.9 %copy-start.546 = (f32[2,512,128]{2,1,0:T(8,128)S(1)}, f32[2,512,128]{2,1,0:T(8,128)}, u32[]{:S(2)}) copy-start(f32[2,512,128]{2,1,0:T(8,128)} %param.30) | copy-start | bytes 1572868
  (570 other events, 1540.4 us)
Sparse Core Ops, SparseCore 0:
  39.4 56.7 all-reduce.321
  193.0 55.6 all-reduce.323
  321.6 28.6 reduce-scatter.2
  357.6 94.0 all-reduce.325
  659.5 19.9 all-gather.6
  681.6 19.8 all-gather.4
  708.1 28.1 reduce-scatter.4
  742.3 94.0 all-reduce.327
  1036.4 19.9 all-gather.10
  1058.5 19.8 all-gather.8
  1082.9 123.1 all-reduce.329
